TPU v7x, 512 devices: a whole 4x8x8 slice. The times are simulated.
512 devices in a mesh: team: 32 (over x_hi, y, core), rep: 16 (over x_lo, z).
Axes of the slice: x: 4 (x_hi: 2, x_lo: 2; x = x_hi * 2 + x_lo), y: 8, z: 8, core: 2. Of those that a mesh axis runs over, the one named last changes fastest.
Arguments:
- points: bfloat16 [32768, 128], P('team'), may hold values from -3 to 3
Outputs:
- potential: float32 [32768], P('team')
- displacement: float32 [32768, 128], P('team')
All inputs are finite; a program needn't handle non-finite values.
Results may differ from a plain program's by a relative error of at most 0.0097.
The roundings to bfloat16 on the way count: a program that leaves them out, or rounds other values in their place, can miss the bound.
Values may be sent and summed in bfloat16 or wider, within the bound.
A program may use at most 64 MiB of HBM per device.

v0:
```python
import jax
import jax.numpy as jnp
from jax import lax
from jax.sharding import PartitionSpec as P


def shards(points):
    rows, width = points.shape
    replicas = lax.axis_size("rep")
    teams = lax.axis_size("team")
    part = rows // replicas
    replica = lax.axis_index("rep")
    log_count = jnp.log(jnp.float32(rows * teams))
    mine = lax.dynamic_slice_in_dim(points, replica * part, part, 0)
    cols = lax.all_gather(mine, "team", axis=0, tiled=True)
    half_rows = 0.5 * jnp.sum(jnp.square(points.astype(jnp.float32)), axis=1)
    half_cols = 0.5 * jnp.sum(jnp.square(cols.astype(jnp.float32)), axis=1)
    products = lax.dot_general(
        points, cols, (((1,), (1,)), ((), ())), preferred_element_type=jnp.float32
    )
    cost = half_rows[:, None] + half_cols[None, :] - products
    first = lax.psum(jnp.sum(jnp.exp(cost * -0.25), axis=1), "rep")
    pot_one = -2.0 * (jnp.log(first) - log_count)
    pot_mine = lax.dynamic_slice_in_dim(pot_one, replica * part, part, 0)
    pot_cols = lax.all_gather(pot_mine, "team", axis=0, tiled=True)
    kernel = jnp.exp((pot_cols[None, :] - cost) * 0.5)
    second_part = jnp.sum(kernel, axis=1)
    numer_part = jnp.dot(kernel.astype(jnp.bfloat16), cols, preferred_element_type=jnp.float32)
    second, numer = lax.psum((second_part, numer_part), "rep")
    potential = 0.5 * (pot_one - 2.0 * (jnp.log(second) - log_count))
    displacement = points.astype(jnp.float32) - numer / second[:, None]
    return (potential, displacement)


def solution(mesh):
    return jax.shard_map(
        shards,
        mesh=mesh,
        in_specs=(P("team", None),),
        out_specs=(P("team"), P("team", None)),
        check_vma=False,
    )
```

profile of v0, /device:TPU:8, one launch (start us, length us, event | category | flops | bytes accessed | tf_op | source)
XLA Modules:
  0.0 313.4 jit_solution(10755890835442421011)
XLA Ops:
  7.2 0.0 all-reduce.3.cloned.1.call-start
  7.2 1.2 fusion.4
  8.4 0.7 constant_dynamic-slice_fusion
  9.1 43.6 %all_gather.6 = bf16[2048,128]{1,0:T(8,128)(2,1)S(1)} all-gather(bf16[64,128]{1,0:T(8,128)(2,1)S(1)} %constant_dynamic-slice_fusion), channel_id=1, replica_groups=mesh['team'=32,'rep'=16] {'team'}, dimensions={0}, use_global_device_ids=true | all-gather | bytes 540672 | tf_op jit(solution)/shard_map/all_gather | solution.py:15
  52.7 0.3 multiply_reduce_fusion
  53.0 5.1 %exponential_reduce_fusion = (f32[1024]{0:T(1024)S(1)}, f32[2048,1024]{1,0:T(8,128)}) fusion(f32[2048]{0:T(1024)S(1)} %broadcast_multiply_fusion, f32[1024]{0:T(1024)S(1)} %broadcast_multiply_fusion.1, bf16[2048,128]{1,0:T(8,128)(2,1)S(1)} %all_gather.6, bf16[1024,128]{1,0:T(8,128)(2,1)} %param.1), kind=kOutput, calls=%fused_computation.2 | convolution fusion | flops 545258496 | bytes 9191424 | tf_op jit(solution)/shard_map/dot_general | solution.py:18
  58.1 36.0 %psum.21 = f32[1024]{0:T(1024)S(1)} all-reduce(f32[1024]{0:T(1024)S(1)} %get-tuple-element.2), channel_id=1, replica_groups=mesh['team'=32,'rep'=16] {'rep'}, use_global_device_ids=true, to_apply=%region_3.0 | all-reduce | flops 1024 | bytes 8192 | tf_op jit(solution)/shard_map/psum | solution.py:22
  94.1 1.3 dynamic-slice
  96.0 0.2 dynamic-slice_dynamic-update-slice_fusion
  96.2 64.4 %all-reduce = f32[2048]{0:T(1024)S(1)} all-reduce(f32[2048]{0:T(1024)S(1)} %dynamic-slice_dynamic-update-slice_fusion), channel_id=1, replica_groups=mesh['team'=32,'rep'=16] {'team'}, use_global_device_ids=true, to_apply=%add | all-reduce | flops 2048 | bytes 16384
  160.6 5.5 %fusion.2 = f32[1024,128]{1,0:T(8,128)} fusion(bf16[2048,128]{1,0:T(8,128)(2,1)S(1)} %all_gather.6, f32[2048,1024]{1,0:T(8,128)} %get-tuple-element.3, f32[2048]{0:T(1024)S(1)} %all-reduce, f32[2048]{0:T(1024)S(1)} %broadcast_multiply_fusion, f32[1024]{0:T(1024)S(1)} %broadcast_multiply_fusion.1), kind=kOutput, calls=%fused_computation.5 | convolution fusion | flops 547356672 | bytes 9457664 | tf_op jit(solution)/shard_map/dot_general | solution.py:28
  166.1 0.0 copy-start
  166.1 0.0 all-reduce.3.cloned.1.call-update
  166.2 4.5 %fusion.1 = f32[1024]{0:T(1024)S(1)} fusion(f32[2048,1024]{1,0:T(8,128)} %get-tuple-element.3, f32[2048]{0:T(1024)S(1)} %all-reduce, f32[2048]{0:T(1024)S(1)} %broadcast_multiply_fusion, f32[1024]{0:T(1024)S(1)} %broadcast_multiply_fusion.1), kind=kLoop, calls=%fused_computation.4 | loop fusion | flops 10484736 | bytes 8413184 | tf_op jit(solution)/shard_map/reduce_sum | solution.py:27
  170.7 30.6 %psum.22 = f32[1024]{0:T(1024)S(1)} all-reduce(f32[1024]{0:T(1024)S(1)} %fusion.1), channel_id=1, replica_groups=mesh['team'=32,'rep'=16] {'rep'}, use_global_device_ids=true, to_apply=%region_5.0 | all-reduce | flops 1024 | bytes 8192 | tf_op jit(solution)/shard_map/psum | solution.py:29
  201.3 0.6 subtract_multiply_fusion
  202.0 102.5 %all-reduce.3.cloned.1.call-done = f32[1024,128]{1,0:T(8,128)} async-done(((f32[1024,128]{1,0:T(8,128)}), f32[1024,128]{1,0:T(8,128)}) %all-reduce.3.cloned.1.call-update) | async-done | bytes 524304 | tf_op jit(solution)/shard_map/psum | solution.py:29
  304.5 0.0 copy-done
  304.5 2.0 convert_subtract_fusion
  (4 shorter events, 0.0 us)
Async XLA Ops:
  7.2 297.3 %all-reduce.3.cloned.1.call-start = ((), (), s32[]{:S(2)}) async-start(), calls=%async_computation | async-start | bytes 1048576 | tf_op jit(solution)/shard_map/psum | solution.py:29
  166.1 138.3 %copy-start = (bf16[1024,128]{1,0:T(8,128)(2,1)S(1)}, bf16[1024,128]{1,0:T(8,128)(2,1)}, u32[]{:S(2)}) copy-start(bf16[1024,128]{1,0:T(8,128)(2,1)} %param.1) | copy-start | bytes 786436
Sparse Core Ops, SparseCore 0:
  166.3 138.1 all-reduce.2
where the time goes:
time: 314 us; the launch traced here: 313 us
  blocking collectives  175 us (56%)
  waiting for transfers between devices  103 us (33%)
  between operations  14.7 us (5%)
  matrix products  10.6 us (3%)
  other arithmetic  8.71 us (3%)
    psum x1, waiting for transfers between devices, shards(): second, numer = lax.psum((second_part, numer_part), 'rep')  103 us
    unnamed x1, blocking collectives  64.4 us
    all_gather x1, blocking collectives, shards(): cols = lax.all_gather(mine, 'team', axis=0, tiled=True)  43.6 us
    psum x1, blocking collectives, shards(): first = lax.psum(jnp.sum(jnp.exp(cost * -0.25), axis=1), 'rep')  36 us
    psum x1, blocking collectives, shards(): second, numer = lax.psum((second_part, numer_part), 'rep')  30.6 us
  transfers between devices with their start and end apart: 1, of which 1 were waited for; matrix products, arithmetic and copies ran while one was open for 2% of the time, Pallas kernels for 0%

commit v1 on v0

--- a/solution.py
+++ b/solution.py
@@ -12,7 +12,9 @@
     replica = lax.axis_index("rep")
     log_count = jnp.log(jnp.float32(rows * teams))
     mine = lax.dynamic_slice_in_dim(points, replica * part, part, 0)
-    cols = lax.all_gather(mine, "team", axis=0, tiled=True)
+    cols = jnp.concatenate(
+        lax.all_to_all(jnp.stack([mine] * lax.axis_size("team")), "team", 0, 0), axis=0
+    )
     half_rows = 0.5 * jnp.sum(jnp.square(points.astype(jnp.float32)), axis=1)
     half_cols = 0.5 * jnp.sum(jnp.square(cols.astype(jnp.float32)), axis=1)
     products = lax.dot_general(

time: 314 us -> 297 us (0.946)
  blocking collectives: 175 us -> 131 us
  waiting for transfers between devices: 103 us -> 118 us
  starting transfers between devices: 0.04 us -> 10.2 us
    all_gather x1 -> x0, blocking collectives: 43.6 us -> none  [shards(): cols = lax.all_gather(mine, 'team', axis=0, tiled=True)]
    all_to_all x0 -> x1, waiting for transfers between devices: none -> 16.1 us  [shards(): lax.all_to_all(jnp.stack([mine] * lax.axis_size('team')), 'team', 0, 0)]
    all_to_all x0 -> x1, starting transfers between devices: none -> 10.2 us  [shards(): lax.all_to_all(jnp.stack([mine] * lax.axis_size('team')), 'team', 0, 0)]
    psum x1, blocking collectives: 36 us -> 39.7 us  [shards(): first = lax.psum(jnp.sum(jnp.exp(cost * -0.25), axis=1), 'rep')]
    unnamed x1, blocking collectives: 64.4 us -> 61 us
  transfers between devices with their start and end apart: 1 -> 2, of which waited for: 1 -> 2; matrix products, arithmetic and copies ran while one was open for 2% -> 3% of each run, Pallas kernels for 0% -> 0%
where the time goes in v1:
time: 297 us
  blocking collectives  131 us (44%)
  waiting for transfers between devices  118 us (40%)
  between operations  14.7 us (5%)
  matrix products  10.6 us (4%)
  starting transfers between devices  10.2 us (3%)
  other arithmetic  8.71 us (3%)
  local copies, waits for them, and re-layouts  3.18 us (1%)
    psum x1, waiting for transfers between devices, shards(): second, numer = lax.psum((second_part, numer_part), 'rep')  102 us
    unnamed x1, blocking collectives  61 us
    psum x1, blocking collectives, shards(): first = lax.psum(jnp.sum(jnp.exp(cost * -0.25), axis=1), 'rep')  39.7 us
    psum x1, blocking collectives, shards(): second, numer = lax.psum((second_part, numer_part), 'rep')  30.6 us
    all_to_all x1, waiting for transfers between devices, shards(): lax.all_to_all(jnp.stack([mine] * lax.axis_size('team')), 'team', 0, 0)  16.1 us
    all_to_all x1, starting transfers between devices, shards(): lax.all_to_all(jnp.stack([mine] * lax.axis_size('team')), 'team', 0, 0)  10.2 us
  transfers between devices with their start and end apart: 2, of which 2 were waited for; matrix products, arithmetic and copies ran while one was open for 3% of the time, Pallas kernels for 0%

profile of v1, /device:TPU:8, one launch (start us, length us, event | category | flops | bytes accessed | tf_op | source)
XLA Modules:
  0.0 296.8 jit_solution(2645927778041121230)
XLA Ops:
  7.2 0.7 constant_dynamic-slice_fusion
  7.9 0.9 stack.2
  8.8 10.2 %all-to-all-start = ((bf16[32,64,128]{2,1,0:T(8,128)(2,1)}), bf16[32,64,128]{2,1,0:T(8,128)(2,1)S(1)}, u32[]{:S(2)}, u32[]{:S(2)}) async-start(bf16[32,64,128]{2,1,0:T(8,128)(2,1)} %stack.2), calls=%async_computation | async-start | bytes 1048576 | tf_op jit(solution)/shard_map/all_to_all | solution.py:16
  19.0 0.0 all-reduce.3.cloned.1.call-start
  19.0 1.3 dynamic-slice
  21.0 1.2 fusion.4
  22.1 16.1 %all-to-all-done = bf16[32,64,128]{2,1,0:T(8,128)(2,1)S(1)} async-done(((bf16[32,64,128]{2,1,0:T(8,128)(2,1)}), bf16[32,64,128]{2,1,0:T(8,128)(2,1)S(1)}, u32[]{:S(2)}, u32[]{:S(2)}) %all-to-all-start) | async-done | bytes 524320 | tf_op jit(solution)/shard_map/all_to_all | solution.py:16
  38.2 0.3 multiply_reduce_fusion
  38.6 0.1 mul.55
  38.6 5.1 %exponential_reduce_fusion = (f32[1024]{0:T(1024)S(1)}, f32[2048,1024]{1,0:T(8,128)}) fusion(f32[2048]{0:T(1024)S(1)} %mul.55, f32[1024]{0:T(1024)S(1)} %broadcast_multiply_fusion.1, bf16[2048,128]{1,0:T(8,128)(2,1)S(1)} %bitcast.16, bf16[1024,128]{1,0:T(8,128)(2,1)} %param.1), kind=kOutput, calls=%fused_computation.2 | convolution fusion | flops 545258496 | bytes 9191424 | tf_op jit(solution)/shard_map/dot_general | solution.py:20
  43.7 39.7 %psum.21 = f32[1024]{0:T(1024)S(1)} all-reduce(f32[1024]{0:T(1024)S(1)} %get-tuple-element.2), channel_id=1, replica_groups=mesh['team'=32,'rep'=16] {'rep'}, use_global_device_ids=true, to_apply=%region_3.0 | all-reduce | flops 1024 | bytes 8192 | tf_op jit(solution)/shard_map/psum | solution.py:24
  83.4 0.2 dynamic-slice_dynamic-update-slice_fusion
  83.6 61.0 %all-reduce = f32[2048]{0:T(1024)S(1)} all-reduce(f32[2048]{0:T(1024)S(1)} %dynamic-slice_dynamic-update-slice_fusion), channel_id=1, replica_groups=mesh['team'=32,'rep'=16] {'team'}, use_global_device_ids=true, to_apply=%add | all-reduce | flops 2048 | bytes 16384
  144.6 5.5 %fusion.2 = f32[1024,128]{1,0:T(8,128)} fusion(bf16[2048,128]{1,0:T(8,128)(2,1)S(1)} %bitcast.17, f32[2048,1024]{1,0:T(8,128)} %get-tuple-element.3, f32[2048]{0:T(1024)S(1)} %all-reduce, f32[2048]{0:T(1024)S(1)} %mul.55, f32[1024]{0:T(1024)S(1)} %broadcast_multiply_fusion.1), kind=kOutput, calls=%fused_computation.5 | convolution fusion | flops 547356672 | bytes 9457664 | tf_op jit(solution)/shard_map/dot_general | solution.py:30
  150.1 0.0 copy-start
  150.1 0.0 all-reduce.3.cloned.1.call-update
  150.2 4.5 %fusion.1 = f32[1024]{0:T(1024)S(1)} fusion(f32[2048,1024]{1,0:T(8,128)} %get-tuple-element.3, f32[2048]{0:T(1024)S(1)} %all-reduce, f32[2048]{0:T(1024)S(1)} %mul.55, f32[1024]{0:T(1024)S(1)} %broadcast_multiply_fusion.1), kind=kLoop, calls=%fused_computation.4 | loop fusion | flops 10484736 | bytes 8413184 | tf_op jit(solution)/shard_map/reduce_sum | solution.py:29
  154.7 30.6 %psum.22 = f32[1024]{0:T(1024)S(1)} all-reduce(f32[1024]{0:T(1024)S(1)} %fusion.1), channel_id=1, replica_groups=mesh['team'=32,'rep'=16] {'rep'}, use_global_device_ids=true, to_apply=%region_5.0 | all-reduce | flops 1024 | bytes 8192 | tf_op jit(solution)/shard_map/psum | solution.py:31
  185.3 0.6 subtract_multiply_fusion
  185.9 101.9 %all-reduce.3.cloned.1.call-done = f32[1024,128]{1,0:T(8,128)} async-done(((f32[1024,128]{1,0:T(8,128)}), f32[1024,128]{1,0:T(8,128)}) %all-reduce.3.cloned.1.call-update) | async-done | bytes 524304 | tf_op jit(solution)/shard_map/psum | solution.py:31
  287.9 0.0 copy-done
  287.9 2.0 convert_subtract_fusion
  (4 shorter events, 0.0 us)
Async XLA Ops:
  8.8 29.4 %all-to-all-start = ((bf16[32,64,128]{2,1,0:T(8,128)(2,1)}), bf16[32,64,128]{2,1,0:T(8,128)(2,1)S(1)}, u32[]{:S(2)}, u32[]{:S(2)}) async-start(bf16[32,64,128]{2,1,0:T(8,128)(2,1)} %stack.2), calls=%async_computation | async-start | bytes 1048576 | tf_op jit(solution)/shard_map/all_to_all | solution.py:16
  19.0 268.9 %all-reduce.3.cloned.1.call-start = ((), (), s32[]{:S(2)}) async-start(), calls=%async_computation.1 | async-start | bytes 1048576 | tf_op jit(solution)/shard_map/psum | solution.py:31
  150.1 137.7 %copy-start = (bf16[1024,128]{1,0:T(8,128)(2,1)S(1)}, bf16[1024,128]{1,0:T(8,128)(2,1)}, u32[]{:S(2)}) copy-start(bf16[1024,128]{1,0:T(8,128)(2,1)} %param.1) | copy-start | bytes 786436
Sparse Core Ops, SparseCore 0:
  150.3 137.5 all-reduce.2
